TPU v7x, 256 devices: a whole 4x4x8 slice. The times are simulated.
256 devices in a mesh: basis: 8 (over z_lo, core), fit: 32 (over z_hi, x, y).
Axes of the slice: x: 4, y: 4, z: 8 (z_hi: 2, z_lo: 4; z = z_hi * 4 + z_lo), core: 2. Of those that a mesh axis runs over, the one named last changes fastest.
Arguments:
- integrals: bfloat16 [1024, 512, 1024], P('basis', 'fit'), may hold values from -6 to 6
- pair_mask: int32 [64, 64], replicated, may hold values 0 or 1
- row_blocks: int32 [64], replicated, may hold values from 0 to 63, each once
- occ_coef: bfloat16 [1024, 64], P('basis'), may hold values from -0.25 to 0.25
- vir_coef: bfloat16 [1024, 32768], P(None, 'fit'), may hold values from -0.1875 to 0.1875
Outputs:
- transformed: bfloat16 [512, 64, 32768], P(None, 'basis', 'fit')
Inputs may be any that keep to these rules, and one draw needn't show every extreme that they name: `row_blocks`: each of the 64 atom blocks appears exactly once. `pair_mask`: 1 marks a significant pair of atom blocks.
All inputs are finite; a program needn't handle non-finite values.
Results may differ from a plain program's by a relative error of at most 0.0049.
Values may be sent and summed in bfloat16 or wider, within the bound.
A program may use at most 128 MiB of HBM per device.

v0:
```python
import jax
import jax.numpy as jnp
from jax import lax
from jax.sharding import PartitionSpec as P

BLK = 16


def shards(integrals, pair_mask, row_blocks, occ_coef, vir_coef):
    mu_dev = integrals.shape[0]
    fit_dev = integrals.shape[1]
    width_nu = integrals.shape[2]
    nocc = occ_coef.shape[1]
    blocks_dev = mu_dev // BLK
    owned = lax.dynamic_slice_in_dim(row_blocks, lax.axis_index("basis") * blocks_dev, blocks_dev)
    panels = lax.all_gather(occ_coef, "basis", axis=0, tiled=True)
    panel_blocks = panels.reshape(-1, BLK, nocc)
    mask_rows = jnp.take(pair_mask, owned, axis=0).astype(jnp.bfloat16)
    mask_full = jnp.repeat(jnp.repeat(mask_rows, BLK, axis=0), BLK, axis=1)
    masked = integrals * mask_full[:, None, :]
    share = nocc // lax.axis_size("basis")
    occ_rows = jnp.take(panel_blocks, owned, axis=0).reshape(mu_dev, nocc)
    flat = masked.reshape(mu_dev, fit_dev * width_nu)
    summed = lax.psum_scatter(
        lax.dot_general(
            occ_rows, flat, (((0,), (0,)), ((), ())), preferred_element_type=jnp.float32
        ),
        "basis",
        scatter_dimension=0,
        tiled=True,
    )
    half = summed.astype(jnp.bfloat16).reshape(share, fit_dev, width_nu)
    product = jnp.einsum(
        "ipn,na->pia",
        lax.all_gather(half, "fit", axis=1, tiled=True),
        vir_coef,
        preferred_element_type=jnp.float32,
    )
    return product.astype(jnp.bfloat16)


def solution(mesh):
    placed = (P("basis", "fit", None), P(), P(), P("basis", None), P(None, "fit"))
    return jax.shard_map(
        shards, mesh=mesh, in_specs=placed, out_specs=P(None, "basis", "fit"), check_vma=False
    )
```

profile of v0, /device:TPU:2, one launch (start us, length us, event | category | flops | bytes accessed | tf_op | source)
XLA Modules:
  0.0 281.8 jit_solution(10232273142838850359)
XLA Ops:
  6.5 0.0 copy-start
  6.5 0.0 reduce-scatter.2.cloned.1.call-start
  6.5 0.9 compare_and_fusion
  7.4 1.3 gather_fusion.1
  8.7 0.1 select_convert_fusion
  8.8 0.1 copy.14
  8.9 0.8 copy.13
  9.8 15.2 %all_gather.6 = bf16[1024,64]{1,0:T(8,128)(2,1)S(1)} all-gather(bf16[128,64]{1,0:T(8,128)(2,1)S(1)} %copy.13), channel_id=1, replica_groups=mesh['basis'=8,'fit'=32] {'basis'}, dimensions={0}, use_global_device_ids=true | all-gather | bytes 147456 | tf_op jit(solution)/shard_map/all_gather | solution.py:16
  24.9 0.6 gather_fusion
  25.5 0.1 broadcast_select_fusion
  25.6 0.1 copy.15
  25.8 2.6 broadcast_multiply_fusion
  28.3 2.7 copy.18
  31.1 2.8 fusion.1
  33.8 0.0 reduce-scatter.2.cloned.1.call-update
  33.9 0.2 all-gather.2.cloned.1.call-start
  34.1 57.2 %reduce-scatter.2.cloned.1.call-done = f32[8,16384]{1,0:T(8,128)} async-done(((f32[64,16384]{1,0:T(8,128)}), f32[8,16384]{1,0:T(8,128)}) %reduce-scatter.2.cloned.1.call-update) | async-done | bytes 524304 | tf_op jit(solution)/shard_map/reduce_scatter | solution.py:24
  91.3 1.1 convert_element_type.13
  92.4 0.9 copy.16
  93.2 0.0 all-gather.2.cloned.1.call-update
  93.3 155.7 %all-gather.2.cloned.1.call-done = bf16[8,512,1024]{2,1,0:T(8,128)(2,1)} async-done(((bf16[8,16,1024]{2,1,0:T(8,128)(2,1)}), bf16[8,512,1024]{2,1,0:T(8,128)(2,1)}) %all-gather.2.cloned.1.call-update) | async-done | bytes 8388624 | tf_op jit(solution)/shard_map/all_gather | solution.py:35
  249.0 0.0 copy-done
  249.0 14.5 %convert_bitcast_fusion = bf16[512,8,1024]{2,0,1:T(8,128)(2,1)} fusion(bf16[8,512,1024]{2,1,0:T(8,128)(2,1)} %all-gather.2.cloned.1.call-done, bf16[1024,1024]{1,0:T(8,128)(2,1)S(1)} %copy-done), kind=kOutput, calls=%fused_computation.2 | convolution fusion | flops 8594128896 | bytes 18874368 | tf_op jit(solution)/shard_map/ipn,na->pia/dot_general | solution.py:33
  263.5 11.5 %copy.17 = bf16[512,8,1024]{2,1,0:T(8,128)(2,1)} copy(bf16[512,8,1024]{2,0,1:T(8,128)(2,1)} %convert_bitcast_fusion) | data formatting | bytes 16777216 | tf_op jit(solution)/shard_map/convert_element_type | solution.py:39
  (3 shorter events, 0.1 us)
Async XLA Ops:
  6.5 242.5 %copy-start = (bf16[1024,1024]{1,0:T(8,128)(2,1)S(1)}, bf16[1024,1024]{1,0:T(8,128)(2,1)}, u32[]{:S(2)}) copy-start(bf16[1024,1024]{1,0:T(8,128)(2,1)} %param.9) | copy-start | bytes 6291460
  6.5 84.8 %reduce-scatter.2.cloned.1.call-start = ((), (), s32[]{:S(2)}) async-start(), calls=%async_computation.1 | async-start | bytes 4718592 | tf_op jit(solution)/shard_map/reduce_scatter | solution.py:24
  33.9 215.1 %all-gather.2.cloned.1.call-start = ((), (), s32[]{:S(2)}) async-start(), calls=%async_computation.2 | async-start | bytes 8650752 | tf_op jit(solution)/shard_map/all_gather | solution.py:35
Sparse Core Ops, SparseCore 0:
  34.0 57.2 reduce-scatter.1
  94.9 154.0 all-gather.1
where the time goes:
time: 283 us; the launch traced here: 282 us
  waiting for transfers between devices  213 us (75%)
  local copies, waits for them, and re-layouts  18.1 us (6%)
  matrix products  17.2 us (6%)
  blocking collectives  15.2 us (5%)
  between operations  13.5 us (5%)
  other arithmetic  4.67 us (2%)
    all_gather x1, waiting for transfers between devices, shards(): lax.all_gather(half, 'fit', axis=1, tiled=True)  156 us
    reduce_scatter x1, waiting for transfers between devices, shards(): lax.psum_scatter(lax.dot_general(occ_rows, flat, (((0,), (0,)), ((), ()))...  57.2 us
    all_gather x1, blocking collectives, shards(): panels = lax.all_gather(occ_coef, 'basis', axis=0, tiled=True)  15.2 us
    dot_general x1, matrix products, shards(): jnp.einsum('ipn,na->pia', lax.all_gather(half, 'fit', axis=1, tiled=True)...  14.5 us
    convert_element_type x1, local copies, waits for them, and re-layouts, shards(): return product.astype(jnp.bfloat16)  11.5 us
  transfers between devices with their start and end apart: 2, of which 2 were waited for; matrix products, arithmetic and copies ran while one was open for 0% of the time, Pallas kernels for 0%

commit v1 on v0

v1 whole, which is shorter than its diff:
```python
import jax
import jax.numpy as jnp
from jax import lax
from jax.experimental import pallas as pl
from jax.experimental.pallas import tpu as pltpu
from jax.sharding import PartitionSpec as P

BLK = 16
NB = 8
NC = 8
N = 1024
HALF = N // 2
F32 = jnp.float32
BF16 = jnp.bfloat16

SIB, Z1, ZH = 0, 1, 4
RING = 5
KINDS = RING + 16
A_UP, A_DN, A_FUP, A_FDN, B_UP, B_DN, B_FUP, B_FDN = range(8)


def kernel(rb_ref, mask_ref, x_hbm, occ_hbm, vir_hbm, out_hbm,
           xv, occ_all, vir, t1, p32, zacc, sib_tx, sib_rx, z_tx, z_rx, g, obuf,
           x_sem, vir_sem, own_sem, out_sem, occ_send, occ_recv, send, recv):
    b = lax.axis_index("basis")
    f = lax.axis_index("fit")
    core, zl = b % 2, b // 2
    zh, x, y = f // 16, (f // 4) % 4, f % 4
    sib = zl * 2 + (1 - core)
    other = (f + 16) % 32
    xp, xm = (x + 1) % 4, (x + 3) % 4
    yp, ym = (y + 1) % 4, (y + 3) % 4
    f_x = (zh * 16 + xp * 4 + y, zh * 16 + xm * 4 + y)
    f_y = (zh * 16 + x * 4 + yp, zh * 16 + x * 4 + ym)

    def remote(src, dst, ssem, rsem, bb, ff):
        return pltpu.make_async_remote_copy(
            src_ref=src, dst_ref=dst, send_sem=ssem, recv_sem=rsem,
            device_id=(bb, ff), device_id_type=pl.DeviceIdType.MESH)

    x_copies = [pltpu.make_async_copy(x_hbm.at[pl.ds(r * 256, 256)], xv.at[pl.ds(r * 256, 256)], x_sem.at[r])
                for r in range(NB)]
    own_copy = pltpu.make_async_copy(occ_hbm, occ_all.at[b], own_sem)
    vir_copy = pltpu.make_async_copy(vir_hbm, vir, vir_sem)
    own_copy.start()
    for c in x_copies:
        c.start()
    vir_copy.start()

    barrier = pltpu.get_barrier_semaphore()
    partners = [((b + d) % NB, f) for d in range(1, NB)] + [(b, other)] + [(b, q) for q in f_x + f_y]
    for bb, ff in partners:
        pl.semaphore_signal(barrier, inc=1, device_id=(bb, ff), device_id_type=pl.DeviceIdType.MESH)
    pl.semaphore_wait(barrier, len(partners))

    def occ_copy(d):
        return remote(occ_hbm, occ_all.at[b], occ_send.at[d - 1], occ_recv.at[d - 1], (b + d) % NB, f)

    def occ_arrival(d):
        slot = occ_all.at[(b + NB - d) % NB]
        return remote(slot, slot, occ_send.at[d - 1], occ_recv.at[d - 1], (b + d) % NB, f)

    for d in range(1, NB):
        occ_copy(d).start()

    owned = [rb_ref[b * NB + r] for r in range(NB)]
    sub8 = lax.broadcasted_iota(jnp.int32, (NB, 64), 0)
    lane64 = lax.broadcasted_iota(jnp.int32, (NB, 64), 1)
    want = jnp.zeros((NB, 64), jnp.int32)
    for r in range(NB):
        want = jnp.where(sub8 == r, owned[r], want)
    pick = jnp.where(lane64 == want, 1.0, 0.0).astype(BF16)
    rows = jnp.dot(pick, mask_ref[...].astype(F32).astype(BF16), preferred_element_type=F32).astype(BF16)
    spread = jnp.where(
        lax.broadcasted_iota(jnp.int32, (64, N), 1) // BLK == lax.broadcasted_iota(jnp.int32, (64, N), 0),
        1.0, 0.0).astype(BF16)
    mask_cols = jnp.dot(rows, spread, preferred_element_type=F32)
    for r in range(NB):
        x_copies[r].wait()
        m = jnp.broadcast_to(mask_cols[r:r + 1, :], (16, N)).astype(BF16)
        for s in range(16):
            at = pl.ds(r * 256 + s * 16, 16)
            xv[at, :] = xv[at, :] * m

    lane_m = lax.broadcasted_iota(jnp.int32, (128, 128), 1)
    source = jnp.zeros((128, 128), jnp.int32)
    for r in range(NB):
        source = jnp.where(lane_m // BLK == r, owned[r] * BLK + lane_m % BLK, source)
    sub_m = lax.broadcasted_iota(jnp.int32, (128, 128), 0)
    own_copy.wait()
    for d in range(1, NB):
        occ_arrival(d).wait_recv()
    occ_sel = jnp.zeros((64, 128), F32)
    for d in range(NB):
        sel = jnp.where(source == sub_m + d * 128, 1.0, 0.0).astype(BF16)
        occ_sel = occ_sel + jnp.dot(occ_all[d], sel, preferred_element_type=F32)
    rep = jnp.where(
        lax.broadcasted_iota(jnp.int32, (128, 2048), 1) // 16 == lax.broadcasted_iota(jnp.int32, (128, 2048), 0),
        1.0, 0.0).astype(BF16)
    t1[...] = jnp.dot(occ_sel.astype(BF16), rep, preferred_element_type=F32)
    vir_copy.wait()

    def sib_copy(c):
        return remote(sib_tx.at[c], sib_rx.at[c], send.at[c, SIB], recv.at[c, SIB], sib, f)

    def z_copy(c, d):
        to = (zl + d) % 4
        return remote(z_tx.at[c, to], z_rx.at[c, d - 1], send.at[c, Z1 + d - 1], recv.at[c, Z1 + d - 1],
                      to * 2 + core, f)

    def zh_copy(c):
        here = g.at[zh, x, y, c]
        return remote(here, here, send.at[c, ZH], recv.at[c, ZH], b, other)

    def zh_arrival(c):
        here = g.at[1 - zh, x, y, c]
        return remote(here, here, send.at[c, ZH], recv.at[c, ZH], b, other)

    def block(k, pos, c):
        return g.at[zh, pos, y, c] if k == 0 else g.at[1 - zh, x, pos, c]

    def group(k, lo, n, pos, c):
        return g.at[zh, pl.ds(lo, n), pos, c] if k == 0 else g.at[1 - zh, pos, pl.ds(lo, n), c]

    def lane_half(ref, h):
        return ref.at[:, pl.ds(h * HALF, HALF)]

    ring1 = ((x, xp, xm, (x + 2) % 4, f_x), (y, yp, ym, (y + 2) % 4, f_y))
    ring2 = (ring1[1], ring1[0])

    def ring_copy(k, j, c, arrival):
        me, up, dn, opp, to = (ring1 if j < B_UP else ring2)[k]
        if j == A_UP:
            ref, dev = block(k, dn if arrival else me, c), to[0]
        elif j == A_DN:
            ref, dev = block(k, up if arrival else me, c), to[1]
        elif j == A_FUP:
            ref, dev = lane_half(block(k, opp if arrival else dn, c), 0), to[0]
        elif j == A_FDN:
            ref, dev = lane_half(block(k, opp if arrival else up, c), 1), to[1]
        elif j == B_UP:
            ref, dev = group(k, 0, 4, dn if arrival else me, c), to[0]
        elif j == B_DN:
            ref, dev = group(k, 0, 4, up if arrival else me, c), to[1]
        elif j == B_FUP:
            ref, dev = group(k, 0, 2, opp if arrival else dn, c), to[0]
        else:
            ref, dev = group(k, 2, 2, opp if arrival else up, c), to[1]
        s = RING + 8 * k + j
        return remote(ref, ref, send.at[c, s], recv.at[c, s], b, dev)

    def go(k, j, c):
        ring_copy(k, j, c, False).start()

    def arrived(k, j, c):
        ring_copy(k, j, c, True).wait_recv()

    col16 = lax.broadcasted_iota(jnp.int32, (8, 2, 8, 2048), 3) % 16
    row2 = lax.broadcasted_iota(jnp.int32, (8, 2, 8, 2048), 1)

    def stage0(c):
        w = jnp.where(col16 == 2 * c + row2, t1[...].reshape(8, 1, 8, 2048), 0.0)
        w = w.reshape(128, 2048).astype(BF16)
        part = jnp.dot(w, xv[...], preferred_element_type=F32)
        p32[...] = part.reshape(4, 2, 16, N)
        sib_tx[c] = p32[:, 1 - core].astype(BF16)
        sib_copy(c).start()
        zacc[c % 2] = p32[:, core]

    def stage1(c):
        sib_copy(c).wait_recv()
        total = zacc[c % 2] + sib_rx[c].astype(F32)
        zacc[c % 2] = total
        z_tx[c] = total.astype(BF16)
        for d in range(1, 4):
            z_copy(c, d).start()

    def stage2(c):
        half = zacc[c % 2, zl]
        for d in range(1, 4):
            z_copy(c, d).wait_recv()
            half = half + z_rx[c, d - 1].astype(F32)
        g[zh, x, y, c] = half.astype(BF16)
        zh_copy(c).start()
        go(0, A_UP, c)
        go(0, A_DN, c)

    def stage3(c):
        zh_arrival(c).wait_recv()
        go(1, A_UP, c)
        go(1, A_DN, c)
        arrived(0, A_UP, c)
        go(0, A_FUP, c)
        arrived(0, A_DN, c)
        go(0, A_FDN, c)

    def stage4(c):
        arrived(0, A_FUP, c)
        arrived(0, A_FDN, c)
        go(0, B_UP, c)
        go(0, B_DN, c)
        arrived(1, A_UP, c)
        go(1, A_FUP, c)
        arrived(1, A_DN, c)
        go(1, A_FDN, c)

    def stage5(c):
        arrived(1, A_FUP, c)
        arrived(1, A_FDN, c)
        go(1, B_UP, c)
        go(1, B_DN, c)
        arrived(0, B_UP, c)
        go(0, B_FUP, c)
        arrived(0, B_DN, c)
        go(0, B_FDN, c)

    def stage6(c):
        arrived(1, B_UP, c)
        go(1, B_FUP, c)
        arrived(1, B_DN, c)
        go(1, B_FDN, c)

    def stage7(c):
        arrived(0, B_FUP, c)
        arrived(0, B_FDN, c)
        arrived(1, B_FUP, c)
        arrived(1, B_FDN, c)

    def out_copy(c):
        return pltpu.make_async_copy(obuf.at[c], out_hbm.at[:, c], out_sem.at[c])

    def stage8(c):
        lhs = g[:, :, :, c].reshape(512, N)
        for q in range(2):
            cols = pl.ds(q * HALF, HALF)
            prod = jnp.dot(lhs, vir[:, cols], preferred_element_type=F32)
            obuf[c, :, :, cols] = prod.astype(BF16).reshape(32, 16, HALF)
        out_copy(c).start()

    stages = (stage7, stage6, stage5, stage4, stage3, stage2, stage1, stage0, stage8)
    lags = (7, 6, 5, 4, 3, 2, 1, 0, 7)

    def step(t, carry):
        for fn, lag in zip(stages, lags):
            c = t - lag

            @pl.when((c >= 0) & (c < NC))
            def _():
                fn(c)
        return carry

    lax.fori_loop(0, NC + 7, step, 0)

    def drain(c, carry):
        sib_copy(c).wait_send()
        for d in range(1, 4):
            z_copy(c, d).wait_send()
        zh_copy(c).wait_send()
        for k in range(2):
            for j in range(8):
                ring_copy(k, j, c, False).wait_send()
        out_copy(c).wait()
        return carry

    lax.fori_loop(0, NC, drain, 0)
    for d in range(1, NB):
        occ_copy(d).wait_send()


def shards(integrals, pair_mask, row_blocks, occ_coef, vir_coef):
    x2 = integrals.reshape(2048, N)
    hbm = pl.BlockSpec(memory_space=pl.ANY)
    out = pl.pallas_call(
        kernel,
        out_shape=jax.ShapeDtypeStruct((32, NC, 16, N), BF16),
        in_specs=[pl.BlockSpec(memory_space=pltpu.SMEM), pl.BlockSpec(memory_space=pltpu.VMEM), hbm, hbm, hbm],
        out_specs=hbm,
        scratch_shapes=[
            pltpu.VMEM((2048, N), BF16),
            pltpu.VMEM((NB, 64, 128), BF16),
            pltpu.VMEM((N, N), BF16),
            pltpu.VMEM((64, 2048), F32),
            pltpu.VMEM((4, 2, 16, N), F32),
            pltpu.VMEM((2, 4, 16, N), F32),
            pltpu.VMEM((NC, 4, 16, N), BF16),
            pltpu.VMEM((NC, 4, 16, N), BF16),
            pltpu.VMEM((NC, 4, 16, N), BF16),
            pltpu.VMEM((NC, 3, 16, N), BF16),
            pltpu.VMEM((2, 4, 4, NC, 16, N), BF16),
            pltpu.VMEM((NC, 32, 16, N), BF16),
            pltpu.SemaphoreType.DMA((NB,)),
            pltpu.SemaphoreType.DMA,
            pltpu.SemaphoreType.DMA,
            pltpu.SemaphoreType.DMA((NC,)),
            pltpu.SemaphoreType.DMA((NB - 1,)),
            pltpu.SemaphoreType.DMA((NB - 1,)),
            pltpu.SemaphoreType.DMA((NC, KINDS)),
            pltpu.SemaphoreType.DMA((NC, KINDS)),
        ],
        compiler_params=pltpu.CompilerParams(
            collective_id=0, has_side_effects=True, vmem_limit_bytes=56 * 2 ** 20),
        cost_estimate=pl.CostEstimate(flops=13 * 10 ** 9, bytes_accessed=15 * 2 ** 20, transcendentals=0),
    )(row_blocks, pair_mask, x2, occ_coef.T, vir_coef)
    return out.reshape(512, 8, N)


def solution(mesh):
    placed = (P("basis", "fit", None), P(), P(), P("basis", None), P(None, "fit"))
    return jax.shard_map(
        shards, mesh=mesh, in_specs=placed, out_specs=P(None, "basis", "fit"), check_vma=False
    )
```

time: 283 us -> 103 us (0.36)
  waiting for transfers between devices: 213 us -> 0 us
  Pallas kernels: 0 us -> 95.5 us
  matrix products: 17.2 us -> 0 us
  blocking collectives: 15.2 us -> 0 us
  between operations: 13.5 us -> 0.01 us
  local copies, waits for them, and re-layouts: 18.1 us -> 7.76 us
  other arithmetic: 4.67 us -> 0 us
    all_gather x1 -> x0, waiting for transfers between devices: 156 us -> none  [shards(): lax.all_gather(half, 'fit', axis=1, tiled=True)]
    pallas_call x0 -> x1, Pallas kernels: none -> 95.5 us  [shards(): pl.pallas_call(kernel, out_shape=jax.ShapeDtypeStruct((32, NC, 16, N), BF...]
    reduce_scatter x1 -> x0, waiting for transfers between devices: 57.2 us -> none  [shards(): lax.psum_scatter(lax.dot_general(occ_rows, flat, (((0,), (0,)), ((), ()))...]
    dot_general x2 -> x0, matrix products: 17.2 us -> none  [the longest x1 14.5 us: shards(): jnp.einsum('ipn,na->pia', lax.all_gather(half, 'fit', axis=1, tiled=True)...]
    all_gather x1 -> x0, blocking collectives: 15.2 us -> none  [shards(): panels = lax.all_gather(occ_coef, 'basis', axis=0, tiled=True)]
    convert_element_type x1 -> x0, local copies, waits for them, and re-layouts: 11.5 us -> none  [shards(): return product.astype(jnp.bfloat16)]
    unnamed x4 -> x1, local copies, waits for them, and re-layouts: 3.59 us -> 7.76 us
  transfers between devices with their start and end apart: 2 -> 0, of which waited for: 2 -> 0; matrix products, arithmetic and copies ran while one was open for 0% -> 0% of each run, Pallas kernels for 0% -> 0%
where the time goes in v1:
time: 103 us
  Pallas kernels  95.5 us (93%)
  local copies, waits for them, and re-layouts  7.76 us (8%)
    pallas_call x1, Pallas kernels, shards(): pl.pallas_call(kernel, out_shape=jax.ShapeDtypeStruct((32, NC, 16, N), BF...  95.5 us
    unnamed x1, local copies, waits for them, and re-layouts  7.76 us

profile of v1, /device:TPU:2, one launch (start us, length us, event | category | flops | bytes accessed | tf_op | source)
XLA Modules:
  0.0 103.3 jit_solution(16099975621901235547)
XLA Ops:
  0.0 95.5 %shard_map.55 = bf16[32,8,16,1024]{3,2,1,0:T(8,128)(2,1)} custom-call(s32[64]{0:T(128)} %rb_ref.1, s32[64,64]{1,0:T(8,128)} %mask_ref.1, bf16[2048,1024]{1,0:T(8,128)(2,1)} %bitcast.4, bf16[64,128]{1,0:T(8,128)(2,1)} %bitcast.5, bf16[1024,1024]{1,0:T(8,128)(2,1)} %vir_hbm.1), custom_call_target="tpu_custom_call" | custom-call | flops 12999999488 | bytes 15728640 | tf_op jit(solution)/shard_map/pallas_call | solution.py:273
  95.5 7.8 %copy.7 = bf16[512,8,1024]{2,1,0:T(8,128)(2,1)} copy(bf16[512,8,1024]{2,1,0:T(8,128)(2,1)} %bitcast.3) | data formatting | bytes 16777216

commit v2 on v1

v2 whole, which is shorter than its diff:
```python
import jax
import jax.numpy as jnp
from jax import lax
from jax.experimental import pallas as pl
from jax.experimental.pallas import tpu as pltpu
from jax.sharding import PartitionSpec as P

BLK = 16
NB = 8
NP = 8
NC = 16
N = 1024
HALF = N // 2
QUART = N // 4
F32 = jnp.float32
BF16 = jnp.bfloat16

SIB, Z1, ZH = 0, 1, 4
RING = 5
KINDS = RING + 16
A_UP, A_DN, A_FUP, A_FDN, B_UP, B_DN, B_FUP, B_FDN = range(8)


def kernel(rb_hbm, mask_hbm, x_hbm, occ_hbm, vir_hbm, done_ref, last_ref, vir,
           rb_ref, mask_ref, xv, occ_all, t1, p32, zacc, sib_tx, sib_rx, z_tx, z_rx, g,
           rb_sem, mask_sem, x_sem, vir_sem, own_sem, occ_send, occ_recv, send, recv):
    b = lax.axis_index("basis")
    f = lax.axis_index("fit")
    core, zl = b % 2, b // 2
    zh, x, y = f // 16, (f // 4) % 4, f % 4
    sib = zl * 2 + (1 - core)
    other = (f + 16) % 32
    xp, xm = (x + 1) % 4, (x + 3) % 4
    yp, ym = (y + 1) % 4, (y + 3) % 4
    f_x = (zh * 16 + xp * 4 + y, zh * 16 + xm * 4 + y)
    f_y = (zh * 16 + x * 4 + yp, zh * 16 + x * 4 + ym)

    def remote(src, dst, ssem, rsem, bb, ff):
        return pltpu.make_async_remote_copy(
            src_ref=src, dst_ref=dst, send_sem=ssem, recv_sem=rsem,
            device_id=(bb, ff), device_id_type=pl.DeviceIdType.MESH)

    barrier = pltpu.get_barrier_semaphore()
    partners = [((b + d) % NB, f) for d in range(1, NB)] + [(b, other)] + [(b, q) for q in f_x + f_y]
    for bb, ff in partners:
        pl.semaphore_signal(barrier, inc=1, device_id=(bb, ff), device_id_type=pl.DeviceIdType.MESH)

    x_copies = [pltpu.make_async_copy(x_hbm.at[pl.ds(r * 256, 256)], xv.at[pl.ds(r * 256, 256)], x_sem.at[r])
                for r in range(NB)]
    own_copy = pltpu.make_async_copy(occ_hbm, occ_all.at[b], own_sem)
    vir_copy = pltpu.make_async_copy(vir_hbm, vir, vir_sem)
    rb_copy = pltpu.make_async_copy(rb_hbm, rb_ref, rb_sem)
    mask_copy = pltpu.make_async_copy(mask_hbm, mask_ref, mask_sem)
    own_copy.start()
    rb_copy.start()
    mask_copy.start()
    for c in x_copies:
        c.start()
    vir_copy.start()

    def occ_copy(d):
        return remote(occ_all.at[b], occ_all.at[b], occ_send.at[d - 1], occ_recv.at[d - 1], (b + d) % NB, f)

    def occ_arrival(d):
        slot = occ_all.at[(b + NB - d) % NB]
        return remote(slot, slot, occ_send.at[d - 1], occ_recv.at[d - 1], (b + d) % NB, f)

    own_copy.wait()
    pl.semaphore_wait(barrier, len(partners))
    for d in range(1, NB):
        occ_copy(d).start()
    rb_copy.wait()
    mask_copy.wait()

    owned = [rb_ref[b * NB + r] for r in range(NB)]
    sub8 = lax.broadcasted_iota(jnp.int32, (NB, 64), 0)
    lane64 = lax.broadcasted_iota(jnp.int32, (NB, 64), 1)
    want = jnp.zeros((NB, 64), jnp.int32)
    for r in range(NB):
        want = jnp.where(sub8 == r, owned[r], want)
    pick = jnp.where(lane64 == want, 1.0, 0.0).astype(BF16)
    rows = jnp.dot(pick, mask_ref[...].astype(F32).astype(BF16), preferred_element_type=F32).astype(BF16)
    spread = jnp.where(
        lax.broadcasted_iota(jnp.int32, (64, N), 1) // BLK == lax.broadcasted_iota(jnp.int32, (64, N), 0),
        1.0, 0.0).astype(BF16)
    mask_cols = jnp.dot(rows, spread, preferred_element_type=F32)
    for r in range(NB):
        x_copies[r].wait()
        m = jnp.broadcast_to(mask_cols[r:r + 1, :], (16, N)).astype(BF16)
        for s in range(16):
            at = pl.ds(r * 256 + s * 16, 16)
            xv[at, :] = xv[at, :] * m

    lane_m = lax.broadcasted_iota(jnp.int32, (128, 128), 1)
    source = jnp.zeros((128, 128), jnp.int32)
    for r in range(NB):
        source = jnp.where(lane_m // BLK == r, owned[r] * BLK + lane_m % BLK, source)
    sub_m = lax.broadcasted_iota(jnp.int32, (128, 128), 0)
    for d in range(1, NB):
        occ_arrival(d).wait_recv()
    occ_sel = jnp.zeros((64, 128), F32)
    for d in range(NB):
        sel = jnp.where(source == sub_m + d * 128, 1.0, 0.0).astype(BF16)
        occ_sel = occ_sel + jnp.dot(occ_all[d], sel, preferred_element_type=F32)
    rep = jnp.where(
        lax.broadcasted_iota(jnp.int32, (128, 2048), 1) // 16 == lax.broadcasted_iota(jnp.int32, (128, 2048), 0),
        1.0, 0.0).astype(BF16)
    t1[...] = jnp.dot(occ_sel.astype(BF16), rep, preferred_element_type=F32)
    vir_copy.wait()

    def sib_copy(c):
        return remote(sib_tx.at[c], sib_rx.at[c], send.at[c, SIB], recv.at[c, SIB], sib, f)

    def z_copy(c, d):
        to = (zl + d) % 4
        return remote(z_tx.at[c, to], z_rx.at[c, d - 1], send.at[c, Z1 + d - 1], recv.at[c, Z1 + d - 1],
                      to * 2 + core, f)

    def zh_copy(c):
        here = g.at[zh, x, y, c // 2, c % 2]
        return remote(here, here, send.at[c, ZH], recv.at[c, ZH], b, other)

    def zh_arrival(c):
        here = g.at[1 - zh, x, y, c // 2, c % 2]
        return remote(here, here, send.at[c, ZH], recv.at[c, ZH], b, other)

    def block(k, pos, c):
        return g.at[zh, pos, y, c // 2, c % 2] if k == 0 else g.at[1 - zh, x, pos, c // 2, c % 2]

    def group(k, lo, n, pos, c):
        if k == 0:
            return g.at[zh, pl.ds(lo, n), pos, c // 2, c % 2]
        return g.at[1 - zh, pos, pl.ds(lo, n), c // 2, c % 2]

    def lane_half(ref, h):
        return ref.at[:, pl.ds(h * QUART, QUART)]

    ring1 = ((x, xp, xm, (x + 2) % 4, f_x), (y, yp, ym, (y + 2) % 4, f_y))
    ring2 = (ring1[1], ring1[0])

    def ring_copy(k, j, c, arrival):
        me, up, dn, opp, to = (ring1 if j < B_UP else ring2)[k]
        if j == A_UP:
            ref, dev = block(k, dn if arrival else me, c), to[0]
        elif j == A_DN:
            ref, dev = block(k, up if arrival else me, c), to[1]
        elif j == A_FUP:
            ref, dev = lane_half(block(k, opp if arrival else dn, c), 0), to[0]
        elif j == A_FDN:
            ref, dev = lane_half(block(k, opp if arrival else up, c), 1), to[1]
        elif j == B_UP:
            ref, dev = group(k, 0, 4, dn if arrival else me, c), to[0]
        elif j == B_DN:
            ref, dev = group(k, 0, 4, up if arrival else me, c), to[1]
        elif j == B_FUP:
            ref, dev = group(k, 0, 2, opp if arrival else dn, c), to[0]
        else:
            ref, dev = group(k, 2, 2, opp if arrival else up, c), to[1]
        s = RING + 8 * k + j
        return remote(ref, ref, send.at[c, s], recv.at[c, s], b, dev)

    def go(k, j, c):
        ring_copy(k, j, c, False).start()

    def arrived(k, j, c):
        ring_copy(k, j, c, True).wait_recv()

    col16 = lax.broadcasted_iota(jnp.int32, (8, 2, 8, 2048), 3) % 16
    row2 = lax.broadcasted_iota(jnp.int32, (8, 2, 8, 2048), 1)

    def stage0(c):
        w = jnp.where(col16 == 2 * (c // 2) + row2, t1[...].reshape(8, 1, 8, 2048), 0.0)
        w = w.reshape(128, 2048).astype(BF16)
        cols = pl.ds(pl.multiple_of((c % 2) * HALF, HALF), HALF)
        part = jnp.dot(w, xv[:, cols], preferred_element_type=F32)
        p32[...] = part.reshape(4, 2, 16, HALF)
        sib_tx[c] = p32[:, 1 - core].astype(BF16)
        sib_copy(c).start()
        zacc[c] = p32[:, core]

    def stage1(c):
        sib_copy(c).wait_recv()
        total = zacc[c] + sib_rx[c].astype(F32)
        zacc[c] = total
        z_tx[c] = total.astype(BF16)
        for d in range(1, 4):
            z_copy(c, d).start()

    def stage2(c):
        half = zacc[c, zl]
        for d in range(1, 4):
            z_copy(c, d).wait_recv()
            half = half + z_rx[c, d - 1].astype(F32)
        g[zh, x, y, c // 2, c % 2] = half.astype(BF16)
        zh_copy(c).start()
        go(0, A_UP, c)
        go(0, A_DN, c)

    def stage3(c):
        zh_arrival(c).wait_recv()
        go(1, A_UP, c)
        go(1, A_DN, c)

    def stage8(c):
        q = c // 2

        @pl.when((c % 2 == 1) & (q < NP - 1))
        def _():
            low = g[:, :, :, q, 0].reshape(512, HALF)
            high = g[:, :, :, q, 1].reshape(512, HALF)
            prod = jnp.dot(low, vir[0:HALF, :], preferred_element_type=F32)
            prod = prod + jnp.dot(high, vir[HALF:N, :], preferred_element_type=F32)
            done_ref[q] = prod.astype(BF16).reshape(32, 16, N)

        @pl.when(c == NC - 1)
        def _():
            for h in range(2):
                last_ref[h] = g[:, :, :, NP - 1, h].reshape(512, HALF)

    def ring_a(k):
        def forward(c):
            arrived(k, A_UP, c)
            go(k, A_FUP, c)
            arrived(k, A_DN, c)
            go(k, A_FDN, c)

        def turn(c):
            arrived(k, A_FUP, c)
            arrived(k, A_FDN, c)
            go(k, B_UP, c)
            go(k, B_DN, c)
        return forward, turn

    def ring_b(k):
        def forward(c):
            arrived(k, B_UP, c)
            go(k, B_FUP, c)
            arrived(k, B_DN, c)
            go(k, B_FDN, c)

        def finish(c):
            arrived(k, B_FUP, c)
            arrived(k, B_FDN, c)
        return forward, finish

    (a20, a30), (a21, a31) = ring_a(0), ring_a(1)
    (a40, a50), (a41, a51) = ring_b(0), ring_b(1)
    schedule = ((a50, 11), (a51, 13), (a41, 11), (a40, 9), (a31, 9), (a30, 7), (a21, 7), (a20, 5), (stage3, 5), (stage2, 3), (stage1, 1), (stage0, 0), (stage8, 13))

    def step(t, carry):
        for fn, lag in schedule:
            c = t - lag

            @pl.when((c >= 0) & (c < NC))
            def _():
                fn(c)
        return carry

    lax.fori_loop(0, NC + max(lag for _, lag in schedule), step, 0)

    def drain(c, carry):
        sib_copy(c).wait_send()
        for d in range(1, 4):
            z_copy(c, d).wait_send()
        zh_copy(c).wait_send()
        for k in range(2):
            for j in range(8):
                ring_copy(k, j, c, False).wait_send()
        return carry

    lax.fori_loop(0, NC, drain, 0)
    for d in range(1, NB):
        occ_copy(d).wait_send()


def finish_kernel(done_ref, last_ref, vir_ref, out_hbm, tail, sem):
    copies = [pltpu.make_async_copy(done_ref.at[q], out_hbm.at[:, q], sem.at[q]) for q in range(NP - 1)]
    for copy in copies:
        copy.start()
    prod = jnp.dot(last_ref[0], vir_ref[0:HALF, :], preferred_element_type=F32)
    prod = prod + jnp.dot(last_ref[1], vir_ref[HALF:N, :], preferred_element_type=F32)
    tail[...] = prod.astype(BF16).reshape(32, 16, N)
    copy = pltpu.make_async_copy(tail, out_hbm.at[:, NP - 1], sem.at[NP - 1])
    copy.start()
    for copy in copies + [copy]:
        copy.wait()


def shards(integrals, pair_mask, row_blocks, occ_coef, vir_coef):
    x2 = integrals.reshape(2048, N)
    hbm = pl.BlockSpec(memory_space=pl.ANY)
    vmem = pl.BlockSpec(memory_space=pltpu.VMEM)
    done, last, vir = pl.pallas_call(
        kernel,
        out_shape=(pltpu.VMEM((NP - 1, 32, 16, N), BF16), pltpu.VMEM((2, 512, HALF), BF16),
                   pltpu.VMEM((N, N), BF16)),
        in_specs=[pl.BlockSpec(memory_space=pltpu.HBM)] * 5,
        out_specs=(vmem, vmem, vmem),
        scratch_shapes=[
            pltpu.SMEM((NB * NB,), jnp.int32),
            pltpu.VMEM((64, 64), jnp.int32),
            pltpu.VMEM((2048, N), BF16),
            pltpu.VMEM((NB, 64, 128), BF16),
            pltpu.VMEM((64, 2048), F32),
            pltpu.VMEM((4, 2, 16, HALF), F32),
            pltpu.VMEM((NC, 4, 16, HALF), F32),
            pltpu.VMEM((NC, 4, 16, HALF), BF16),
            pltpu.VMEM((NC, 4, 16, HALF), BF16),
            pltpu.VMEM((NC, 4, 16, HALF), BF16),
            pltpu.VMEM((NC, 3, 16, HALF), BF16),
            pltpu.VMEM((2, 4, 4, NP, 2, 16, HALF), BF16),
            pltpu.SemaphoreType.DMA,
            pltpu.SemaphoreType.DMA,
            pltpu.SemaphoreType.DMA((NB,)),
            pltpu.SemaphoreType.DMA,
            pltpu.SemaphoreType.DMA,
            pltpu.SemaphoreType.DMA((NB - 1,)),
            pltpu.SemaphoreType.DMA((NB - 1,)),
            pltpu.SemaphoreType.DMA((NC, KINDS)),
            pltpu.SemaphoreType.DMA((NC, KINDS)),
        ],
        compiler_params=pltpu.CompilerParams(
            collective_id=0, has_side_effects=True, vmem_limit_bytes=53900 * 1024),
        cost_estimate=pl.CostEstimate(flops=13 * 10 ** 9, bytes_accessed=15 * 2 ** 20, transcendentals=0),
    )(row_blocks, pair_mask, x2, occ_coef.T, vir_coef)
    out = pl.pallas_call(
        finish_kernel,
        out_shape=jax.ShapeDtypeStruct((32, NP, 16, N), BF16),
        in_specs=[vmem, vmem, vmem],
        out_specs=hbm,
        scratch_shapes=[pltpu.VMEM((32, 16, N), BF16), pltpu.SemaphoreType.DMA((NP,))],
        compiler_params=pltpu.CompilerParams(vmem_limit_bytes=12 * 2 ** 20),
    )(done, last, vir)
    return out.reshape(512, 8, N)


def solution(mesh):
    placed = (P("basis", "fit", None), P(), P(), P("basis", None), P(None, "fit"))
    return jax.shard_map(
        shards, mesh=mesh, in_specs=placed, out_specs=P(None, "basis", "fit"), check_vma=False
    )
```

time: 103 us -> 88.2 us (0.86)
  local copies, waits for them, and re-layouts: 7.76 us -> 0 us
  Pallas kernels: 95.5 us -> 88.1 us
    unnamed x1 -> x0, local copies, waits for them, and re-layouts: 7.76 us -> none
    pallas_call x1 -> x2, Pallas kernels: 95.5 us -> 88.1 us  [the longest x1 84.7 us: shards(): pl.pallas_call(kernel, out_shape=(pltpu.VMEM((NP - 1, 32, 16, N), BF16),...]
where the time goes in v2:
time: 88.2 us; the launch traced here: 88.1 us
  Pallas kernels  88.1 us (100%)
    pallas_call x1, Pallas kernels, shards(): pl.pallas_call(kernel, out_shape=(pltpu.VMEM((NP - 1, 32, 16, N), BF16),...  84.7 us
    pallas_call x1, Pallas kernels, shards(): pl.pallas_call(finish_kernel, out_shape=jax.ShapeDtypeStruct((32, NP, 16,...  3.4 us

profile of v2, /device:TPU:2, one launch (start us, length us, event | category | flops | bytes accessed | tf_op | source)
XLA Modules:
  0.0 88.1 jit_solution(3309987050091242838)
XLA Ops:
  0.0 84.7 %shard_map.55 = (bf16[7,32,16,1024]{3,2,1,0:T(8,128)(2,1)S(1)}, bf16[2,512,512]{2,1,0:T(8,128)(2,1)S(1)}, bf16[1024,1024]{1,0:T(8,128)(2,1)S(1)}) custom-call(s32[64]{0:T(128)} %rb_hbm.1, s32[64,64]{1,0:T(8,128)} %mask_hbm.1, bf16[2048,1024]{1,0:T(8,128)(2,1)} %bitcast.3, bf16[64,128]{1,0:T(8,128)(2,1)} %bitcast.4, bf16[1024,1024]{1,0:T(8,128)(2,1)} %vir_hbm.1), custom_call_target="tpu_custom_call" | custom-call | flops 12999999488 | bytes 15728640 | tf_op jit(solution)/shard_map/pallas_call | solution.py:293
  84.7 3.4 %shard_map.56 = bf16[32,8,16,1024]{3,2,1,0:T(8,128)(2,1)} custom-call(bf16[7,32,16,1024]{3,2,1,0:T(8,128)(2,1)S(1)} %get-tuple-element.8.done_ref, bf16[2,512,512]{2,1,0:T(8,128)(2,1)S(1)} %get-tuple-element.9.last_ref, bf16[1024,1024]{1,0:T(8,128)(2,1)S(1)} %get-tuple-element.10.vir_ref), custom_call_target="tpu_custom_call" | custom-call | tf_op jit(solution)/shard_map/pallas_call | solution.py:326

commit v3 on v2

--- a/solution.py
+++ b/solution.py
@@ -8,7 +8,7 @@
 BLK = 16
 NB = 8
 NP = 8
-NC = 16
+NC = 8
 N = 1024
 HALF = N // 2
 QUART = N // 4
@@ -17,8 +17,13 @@
 
 SIB, Z1, ZH = 0, 1, 4
 RING = 5
-KINDS = RING + 16
-A_UP, A_DN, A_FUP, A_FDN, B_UP, B_DN, B_FUP, B_FDN = range(8)
+PER_STREAM = 12
+KINDS = RING + 4 * PER_STREAM
+A_UP, A_DN, A_FUP, A_FDN, B0_UP, B0_DN, B1_UP, B1_DN, B2_UP, B2_DN, B_FUP, B_FDN = range(PER_STREAM)
+ME, UP, DN, OPP = range(4)
+FIRST = {A_UP: (ME, DN), A_DN: (ME, UP), A_FUP: (DN, OPP), A_FDN: (UP, OPP)}
+SECOND = {B0_UP: (ME, DN, 0, 1), B0_DN: (ME, UP, 0, 1), B1_UP: (ME, DN, 1, 2), B1_DN: (ME, UP, 1, 2),
+          B2_UP: (ME, DN, 3, 1), B2_DN: (ME, UP, 3, 1), B_FUP: (DN, OPP, 0, 2), B_FDN: (UP, OPP, 2, 2)}
 
 
 def kernel(rb_hbm, mask_hbm, x_hbm, occ_hbm, vir_hbm, done_ref, last_ref, vir,
@@ -117,63 +122,52 @@
                       to * 2 + core, f)
 
     def zh_copy(c):
-        here = g.at[zh, x, y, c // 2, c % 2]
-        return remote(here, here, send.at[c, ZH], recv.at[c, ZH], b, other)
-
-    def zh_arrival(c):
-        here = g.at[1 - zh, x, y, c // 2, c % 2]
-        return remote(here, here, send.at[c, ZH], recv.at[c, ZH], b, other)
-
-    def block(k, pos, c):
-        return g.at[zh, pos, y, c // 2, c % 2] if k == 0 else g.at[1 - zh, x, pos, c // 2, c % 2]
-
-    def group(k, lo, n, pos, c):
-        if k == 0:
-            return g.at[zh, pl.ds(lo, n), pos, c // 2, c % 2]
-        return g.at[1 - zh, pos, pl.ds(lo, n), c // 2, c % 2]
+        return remote(g.at[0, c, :, ME, ME], g.at[1, c, :, ME, ME], send.at[c, ZH], recv.at[c, ZH], b, other)
+
+    def along_x(k, h):
+        return (k + h) % 2 == 0
+
+    def block(k, h, pos, c):
+        return g.at[k, c, h, pos, ME] if along_x(k, h) else g.at[k, c, h, ME, pos]
+
+    def group(k, h, lo, n, pos, c):
+        if along_x(k, h):
+            return g.at[k, c, h, pl.ds(lo, n), pos]
+        return g.at[k, c, h, pos, pl.ds(lo, n)]
 
     def lane_half(ref, h):
         return ref.at[:, pl.ds(h * QUART, QUART)]
 
-    ring1 = ((x, xp, xm, (x + 2) % 4, f_x), (y, yp, ym, (y + 2) % 4, f_y))
-    ring2 = (ring1[1], ring1[0])
-
-    def ring_copy(k, j, c, arrival):
-        me, up, dn, opp, to = (ring1 if j < B_UP else ring2)[k]
-        if j == A_UP:
-            ref, dev = block(k, dn if arrival else me, c), to[0]
-        elif j == A_DN:
-            ref, dev = block(k, up if arrival else me, c), to[1]
-        elif j == A_FUP:
-            ref, dev = lane_half(block(k, opp if arrival else dn, c), 0), to[0]
-        elif j == A_FDN:
-            ref, dev = lane_half(block(k, opp if arrival else up, c), 1), to[1]
-        elif j == B_UP:
-            ref, dev = group(k, 0, 4, dn if arrival else me, c), to[0]
-        elif j == B_DN:
-            ref, dev = group(k, 0, 4, up if arrival else me, c), to[1]
-        elif j == B_FUP:
-            ref, dev = group(k, 0, 2, opp if arrival else dn, c), to[0]
+    def ring_copy(k, h, j, c, arrival):
+        if j in FIRST:
+            source, target = FIRST[j]
+            src, dst = block(k, h, source, c), block(k, h, target, c)
+            if j in (A_FUP, A_FDN):
+                src, dst = lane_half(src, j - A_FUP), lane_half(dst, j - A_FUP)
         else:
-            ref, dev = group(k, 2, 2, opp if arrival else up, c), to[1]
-        s = RING + 8 * k + j
-        return remote(ref, ref, send.at[c, s], recv.at[c, s], b, dev)
-
-    def go(k, j, c):
-        ring_copy(k, j, c, False).start()
-
-    def arrived(k, j, c):
-        ring_copy(k, j, c, True).wait_recv()
+            source, target, lo, n = SECOND[j]
+            src, dst = group(k, h, lo, n, source, c), group(k, h, lo, n, target, c)
+        to = f_x if along_x(k, h) == (j in FIRST) else f_y
+        dev = to[0] if j in (A_UP, A_FUP, B0_UP, B1_UP, B2_UP, B_FUP) else to[1]
+        s = RING + PER_STREAM * (2 * k + h) + j
+        return remote(dst if arrival else src, dst, send.at[c, s], recv.at[c, s], b, dev)
+
+    def go(k, j, c, h):
+        ring_copy(k, h, j, c, False).start()
+
+    def arrived(k, j, c, h):
+        ring_copy(k, h, j, c, True).wait_recv()
 
     col16 = lax.broadcasted_iota(jnp.int32, (8, 2, 8, 2048), 3) % 16
     row2 = lax.broadcasted_iota(jnp.int32, (8, 2, 8, 2048), 1)
 
     def stage0(c):
-        w = jnp.where(col16 == 2 * (c // 2) + row2, t1[...].reshape(8, 1, 8, 2048), 0.0)
+        w = jnp.where(col16 == 2 * c + row2, t1[...].reshape(8, 1, 8, 2048), 0.0)
         w = w.reshape(128, 2048).astype(BF16)
-        cols = pl.ds(pl.multiple_of((c % 2) * HALF, HALF), HALF)
-        part = jnp.dot(w, xv[:, cols], preferred_element_type=F32)
-        p32[...] = part.reshape(4, 2, 16, HALF)
+        for h in range(2):
+            cols = pl.ds(h * HALF, HALF)
+            part = jnp.dot(w, xv[:, cols], preferred_element_type=F32)
+            p32[:, :, :, cols] = part.reshape(4, 2, 16, HALF)
         sib_tx[c] = p32[:, 1 - core].astype(BF16)
         sib_copy(c).start()
         zacc[c] = p32[:, core]
@@ -191,61 +185,82 @@
         for d in range(1, 4):
             z_copy(c, d).wait_recv()
             half = half + z_rx[c, d - 1].astype(F32)
-        g[zh, x, y, c // 2, c % 2] = half.astype(BF16)
+        for h in range(2):
+            g[0, c, h, ME, ME] = half[:, h * HALF:(h + 1) * HALF].astype(BF16)
         zh_copy(c).start()
-        go(0, A_UP, c)
-        go(0, A_DN, c)
+        for h in range(2):
+            go(0, A_UP, c, h)
+            go(0, A_DN, c, h)
+            go(0, B0_UP, c, h)
+            go(0, B0_DN, c, h)
 
     def stage3(c):
-        zh_arrival(c).wait_recv()
-        go(1, A_UP, c)
-        go(1, A_DN, c)
+        zh_copy(c).wait_recv()
+        for h in range(2):
+            go(1, A_UP, c, h)
+            go(1, A_DN, c, h)
+            go(1, B0_UP, c, h)
+            go(1, B0_DN, c, h)
+
+    xo, yo = (x + 2) % 4, (y + 2) % 4
+    places = [(k, i, j, plane * 16 + px * 4 + py)
+              for k, plane in ((0, zh), (1, 1 - zh))
+              for i, px in enumerate((x, xp, xm, xo)) for j, py in enumerate((y, yp, ym, yo))]
 
     def stage8(c):
-        q = c // 2
-
-        @pl.when((c % 2 == 1) & (q < NP - 1))
+        @pl.when(c < NP - 1)
         def _():
-            low = g[:, :, :, q, 0].reshape(512, HALF)
-            high = g[:, :, :, q, 1].reshape(512, HALF)
+            low = g[:, c, 0].reshape(512, HALF)
+            high = g[:, c, 1].reshape(512, HALF)
             prod = jnp.dot(low, vir[0:HALF, :], preferred_element_type=F32)
             prod = prod + jnp.dot(high, vir[HALF:N, :], preferred_element_type=F32)
-            done_ref[q] = prod.astype(BF16).reshape(32, 16, N)
-
-        @pl.when(c == NC - 1)
+            prod = prod.astype(BF16)
+            for n, (_, _, _, at) in enumerate(places):
+                done_ref[c, at] = prod[n * 16:(n + 1) * 16]
+
+        @pl.when(c == NP - 1)
         def _():
-            for h in range(2):
-                last_ref[h] = g[:, :, :, NP - 1, h].reshape(512, HALF)
-
-    def ring_a(k):
-        def forward(c):
-            arrived(k, A_UP, c)
-            go(k, A_FUP, c)
-            arrived(k, A_DN, c)
-            go(k, A_FDN, c)
+            for k, i, j, at in places:
+                for h in range(2):
+                    last_ref[h, at] = g[k, NP - 1, h, i, j]
+
+    def ring(k):
+        def forward_first(c):
+            for h in range(2):
+                arrived(k, A_UP, c, h)
+                go(k, A_FUP, c, h)
+                arrived(k, A_DN, c, h)
+                go(k, A_FDN, c, h)
+                go(k, B1_UP, c, h)
+                go(k, B1_DN, c, h)
 
         def turn(c):
-            arrived(k, A_FUP, c)
-            arrived(k, A_FDN, c)
-            go(k, B_UP, c)
-            go(k, B_DN, c)
-        return forward, turn
-
-    def ring_b(k):
-        def forward(c):
-            arrived(k, B_UP, c)
-            go(k, B_FUP, c)
-            arrived(k, B_DN, c)
-            go(k, B_FDN, c)
+            for h in range(2):
+                arrived(k, A_FUP, c, h)
+                arrived(k, A_FDN, c, h)
+                go(k, B2_UP, c, h)
+                go(k, B2_DN, c, h)
+
+        def forward_up(c):
+            for h in range(2):
+                arrived(k, B0_UP, c, h)
+                arrived(k, B1_UP, c, h)
+                go(k, B_FUP, c, h)
+
+        def forward_down(c):
+            for h in range(2):
+                arrived(k, B1_DN, c, h)
+                arrived(k, B2_DN, c, h)
+                go(k, B_FDN, c, h)
 
         def finish(c):
-            arrived(k, B_FUP, c)
-            arrived(k, B_FDN, c)
-        return forward, finish
-
-    (a20, a30), (a21, a31) = ring_a(0), ring_a(1)
-    (a40, a50), (a41, a51) = ring_b(0), ring_b(1)
-    schedule = ((a50, 11), (a51, 13), (a41, 11), (a40, 9), (a31, 9), (a30, 7), (a21, 7), (a20, 5), (stage3, 5), (stage2, 3), (stage1, 1), (stage0, 0), (stage8, 13))
+            for h in range(2):
+                for j in (B0_DN, B2_UP, B_FUP, B_FDN):
+                    arrived(k, j, c, h)
+        return forward_first, turn, forward_up, forward_down, finish
+
+    (a20, a30, a40, a60, a50), (a21, a31, a41, a61, a51) = ring(0), ring(1)
+    schedule = ((stage0, 0), (stage1, 0), (stage2, 1), (a20, 2), (a40, 3), (a30, 3), (a60, 4), (stage3, 2), (a21, 3), (a41, 4), (a31, 4), (a61, 5), (a50, 6), (a51, 7), (stage8, 7))
 
     def step(t, carry):
         for fn, lag in schedule:
@@ -264,8 +279,9 @@
             z_copy(c, d).wait_send()
         zh_copy(c).wait_send()
         for k in range(2):
-            for j in range(8):
-                ring_copy(k, j, c, False).wait_send()
+            for h in range(2):
+                for j in range(PER_STREAM):
+                    ring_copy(k, h, j, c, False).wait_send()
         return carry
 
     lax.fori_loop(0, NC, drain, 0)
@@ -277,8 +293,9 @@
     copies = [pltpu.make_async_copy(done_ref.at[q], out_hbm.at[:, q], sem.at[q]) for q in range(NP - 1)]
     for copy in copies:
         copy.start()
-    prod = jnp.dot(last_ref[0], vir_ref[0:HALF, :], preferred_element_type=F32)
-    prod = prod + jnp.dot(last_ref[1], vir_ref[HALF:N, :], preferred_element_type=F32)
+    low, high = last_ref[0].reshape(512, HALF), last_ref[1].reshape(512, HALF)
+    prod = jnp.dot(low, vir_ref[0:HALF, :], preferred_element_type=F32)
+    prod = prod + jnp.dot(high, vir_ref[HALF:N, :], preferred_element_type=F32)
     tail[...] = prod.astype(BF16).reshape(32, 16, N)
     copy = pltpu.make_async_copy(tail, out_hbm.at[:, NP - 1], sem.at[NP - 1])
     copy.start()
@@ -292,7 +309,7 @@
     vmem = pl.BlockSpec(memory_space=pltpu.VMEM)
     done, last, vir = pl.pallas_call(
         kernel,
-        out_shape=(pltpu.VMEM((NP - 1, 32, 16, N), BF16), pltpu.VMEM((2, 512, HALF), BF16),
+        out_shape=(pltpu.VMEM((NP - 1, 32, 16, N), BF16), pltpu.VMEM((2, 32, 16, HALF), BF16),
                    pltpu.VMEM((N, N), BF16)),
         in_specs=[pl.BlockSpec(memory_space=pltpu.HBM)] * 5,
         out_specs=(vmem, vmem, vmem),
@@ -302,13 +319,13 @@
             pltpu.VMEM((2048, N), BF16),
             pltpu.VMEM((NB, 64, 128), BF16),
             pltpu.VMEM((64, 2048), F32),
-            pltpu.VMEM((4, 2, 16, HALF), F32),
-            pltpu.VMEM((NC, 4, 16, HALF), F32),
-            pltpu.VMEM((NC, 4, 16, HALF), BF16),
-            pltpu.VMEM((NC, 4, 16, HALF), BF16),
-            pltpu.VMEM((NC, 4, 16, HALF), BF16),
-            pltpu.VMEM((NC, 3, 16, HALF), BF16),
-            pltpu.VMEM((2, 4, 4, NP, 2, 16, HALF), BF16),
+            pltpu.VMEM((4, 2, 16, N), F32),
+            pltpu.VMEM((NC, 4, 16, N), F32),
+            pltpu.VMEM((NC, 4, 16, N), BF16),
+            pltpu.VMEM((NC, 4, 16, N), BF16),
+            pltpu.VMEM((NC, 4, 16, N), BF16),
+            pltpu.VMEM((NC, 3, 16, N), BF16),
+            pltpu.VMEM((2, NP, 2, 4, 4, 16, HALF), BF16),
             pltpu.SemaphoreType.DMA,
             pltpu.SemaphoreType.DMA,
             pltpu.SemaphoreType.DMA((NB,)),

time: 88.2 us -> 86.3 us (0.978)
  Pallas kernels: 88.1 us -> 85.8 us
    pallas_call x1, Pallas kernels: 84.7 us -> 82.4 us  [shards(): pl.pallas_call(kernel, out_shape=(pltpu.VMEM((NP - 1, 32, 16, N), BF16),...]
where the time goes in v3:
time: 86.3 us; the launch traced here: 85.8 us
  Pallas kernels  85.8 us (99%)
    pallas_call x1, Pallas kernels, shards(): pl.pallas_call(kernel, out_shape=(pltpu.VMEM((NP - 1, 32, 16, N), BF16),...  82.4 us
    pallas_call x1, Pallas kernels, shards(): pl.pallas_call(finish_kernel, out_shape=jax.ShapeDtypeStruct((32, NP, 16,...  3.4 us

profile of v3, /device:TPU:2, one launch (start us, length us, event | category | flops | bytes accessed | tf_op | source)
XLA Modules:
  0.0 85.8 jit_solution(3831455226429005026)
XLA Ops:
  0.0 82.4 %shard_map.55 = (bf16[7,32,16,1024]{3,2,1,0:T(8,128)(2,1)S(1)}, bf16[2,32,16,512]{3,2,1,0:T(8,128)(2,1)S(1)}, bf16[1024,1024]{1,0:T(8,128)(2,1)S(1)}) custom-call(s32[64]{0:T(128)} %rb_hbm.1, s32[64,64]{1,0:T(8,128)} %mask_hbm.1, bf16[2048,1024]{1,0:T(8,128)(2,1)} %bitcast.3, bf16[64,128]{1,0:T(8,128)(2,1)} %bitcast.4, bf16[1024,1024]{1,0:T(8,128)(2,1)} %vir_hbm.1), custom_call_target="tpu_custom_call" | custom-call | flops 12999999488 | bytes 15728640 | tf_op jit(solution)/shard_map/pallas_call | solution.py:310
  82.4 3.4 %shard_map.56 = bf16[32,8,16,1024]{3,2,1,0:T(8,128)(2,1)} custom-call(bf16[7,32,16,1024]{3,2,1,0:T(8,128)(2,1)S(1)} %get-tuple-element.8.done_ref, bf16[2,32,16,512]{3,2,1,0:T(8,128)(2,1)S(1)} %get-tuple-element.9.last_ref, bf16[1024,1024]{1,0:T(8,128)(2,1)S(1)} %get-tuple-element.10.vir_ref), custom_call_target="tpu_custom_call" | custom-call | tf_op jit(solution)/shard_map/pallas_call | solution.py:343

commit v4 on v3

--- a/solution.py
+++ b/solution.py
@@ -15,8 +15,8 @@
 F32 = jnp.float32
 BF16 = jnp.bfloat16
 
-SIB, Z1, ZH = 0, 1, 4
-RING = 5
+SIB, Z1, ZH = 0, 2, 8
+RING = 10
 PER_STREAM = 12
 KINDS = RING + 4 * PER_STREAM
 A_UP, A_DN, A_FUP, A_FDN, B0_UP, B0_DN, B1_UP, B1_DN, B2_UP, B2_DN, B_FUP, B_FDN = range(PER_STREAM)
@@ -111,18 +111,17 @@
         lax.broadcasted_iota(jnp.int32, (128, 2048), 1) // 16 == lax.broadcasted_iota(jnp.int32, (128, 2048), 0),
         1.0, 0.0).astype(BF16)
     t1[...] = jnp.dot(occ_sel.astype(BF16), rep, preferred_element_type=F32)
-    vir_copy.wait()
-
-    def sib_copy(c):
-        return remote(sib_tx.at[c], sib_rx.at[c], send.at[c, SIB], recv.at[c, SIB], sib, f)
-
-    def z_copy(c, d):
+
+    def sib_copy(c, h):
+        return remote(sib_tx.at[c, h], sib_rx.at[c, h], send.at[c, SIB + h], recv.at[c, SIB + h], sib, f)
+
+    def z_copy(c, d, h):
         to = (zl + d) % 4
-        return remote(z_tx.at[c, to], z_rx.at[c, d - 1], send.at[c, Z1 + d - 1], recv.at[c, Z1 + d - 1],
-                      to * 2 + core, f)
-
-    def zh_copy(c):
-        return remote(g.at[0, c, :, ME, ME], g.at[1, c, :, ME, ME], send.at[c, ZH], recv.at[c, ZH], b, other)
+        s = Z1 + 3 * h + d - 1
+        return remote(z_tx.at[c, h, to], z_rx.at[c, h, d - 1], send.at[c, s], recv.at[c, s], to * 2 + core, f)
+
+    def zh_copy(c, h):
+        return remote(g.at[0, c, h, ME, ME], g.at[1, c, h, ME, ME], send.at[c, ZH + h], recv.at[c, ZH + h], b, other)
 
     def along_x(k, h):
         return (k + h) % 2 == 0
@@ -167,36 +166,35 @@
         for h in range(2):
             cols = pl.ds(h * HALF, HALF)
             part = jnp.dot(w, xv[:, cols], preferred_element_type=F32)
-            p32[:, :, :, cols] = part.reshape(4, 2, 16, HALF)
-        sib_tx[c] = p32[:, 1 - core].astype(BF16)
-        sib_copy(c).start()
-        zacc[c] = p32[:, core]
+            p32[h] = part.reshape(4, 2, 16, HALF)
+            sib_tx[c, h] = p32[h, :, 1 - core].astype(BF16)
+            sib_copy(c, h).start()
 
     def stage1(c):
-        sib_copy(c).wait_recv()
-        total = zacc[c] + sib_rx[c].astype(F32)
-        zacc[c] = total
-        z_tx[c] = total.astype(BF16)
-        for d in range(1, 4):
-            z_copy(c, d).start()
+        for h in range(2):
+            sib_copy(c, h).wait_recv()
+            total = p32[h, :, core] + sib_rx[c, h].astype(F32)
+            zacc[c, h] = total
+            z_tx[c, h] = total.astype(BF16)
+            for d in range(1, 4):
+                z_copy(c, d, h).start()
 
     def stage2(c):
-        half = zacc[c, zl]
-        for d in range(1, 4):
-            z_copy(c, d).wait_recv()
-            half = half + z_rx[c, d - 1].astype(F32)
-        for h in range(2):
-            g[0, c, h, ME, ME] = half[:, h * HALF:(h + 1) * HALF].astype(BF16)
-        zh_copy(c).start()
-        for h in range(2):
+        for h in range(2):
+            half = zacc[c, h, zl]
+            for d in range(1, 4):
+                z_copy(c, d, h).wait_recv()
+                half = half + z_rx[c, h, d - 1].astype(F32)
+            g[0, c, h, ME, ME] = half.astype(BF16)
+            zh_copy(c, h).start()
             go(0, A_UP, c, h)
             go(0, A_DN, c, h)
             go(0, B0_UP, c, h)
             go(0, B0_DN, c, h)
 
     def stage3(c):
-        zh_copy(c).wait_recv()
-        for h in range(2):
+        for h in range(2):
+            zh_copy(c, h).wait_recv()
             go(1, A_UP, c, h)
             go(1, A_DN, c, h)
             go(1, B0_UP, c, h)
@@ -263,6 +261,10 @@
     schedule = ((stage0, 0), (stage1, 0), (stage2, 1), (a20, 2), (a40, 3), (a30, 3), (a60, 4), (stage3, 2), (a21, 3), (a41, 4), (a31, 4), (a61, 5), (a50, 6), (a51, 7), (stage8, 7))
 
     def step(t, carry):
+        @pl.when(t == 3)
+        def _():
+            vir_copy.wait()
+
         for fn, lag in schedule:
             c = t - lag
 
@@ -274,10 +276,11 @@
     lax.fori_loop(0, NC + max(lag for _, lag in schedule), step, 0)
 
     def drain(c, carry):
-        sib_copy(c).wait_send()
-        for d in range(1, 4):
-            z_copy(c, d).wait_send()
-        zh_copy(c).wait_send()
+        for h in range(2):
+            sib_copy(c, h).wait_send()
+            for d in range(1, 4):
+                z_copy(c, d, h).wait_send()
+            zh_copy(c, h).wait_send()
         for k in range(2):
             for h in range(2):
                 for j in range(PER_STREAM):
@@ -319,12 +322,12 @@
             pltpu.VMEM((2048, N), BF16),
             pltpu.VMEM((NB, 64, 128), BF16),
             pltpu.VMEM((64, 2048), F32),
-            pltpu.VMEM((4, 2, 16, N), F32),
-            pltpu.VMEM((NC, 4, 16, N), F32),
-            pltpu.VMEM((NC, 4, 16, N), BF16),
-            pltpu.VMEM((NC, 4, 16, N), BF16),
-            pltpu.VMEM((NC, 4, 16, N), BF16),
-            pltpu.VMEM((NC, 3, 16, N), BF16),
+            pltpu.VMEM((2, 4, 2, 16, HALF), F32),
+            pltpu.VMEM((NC, 2, 4, 16, HALF), F32),
+            pltpu.VMEM((NC, 2, 4, 16, HALF), BF16),
+            pltpu.VMEM((NC, 2, 4, 16, HALF), BF16),
+            pltpu.VMEM((NC, 2, 4, 16, HALF), BF16),
+            pltpu.VMEM((NC, 2, 3, 16, HALF), BF16),
             pltpu.VMEM((2, NP, 2, 4, 4, 16, HALF), BF16),
             pltpu.SemaphoreType.DMA,
             pltpu.SemaphoreType.DMA,

time: 86.3 us -> 86.7 us (level)
  no operation moved by 1% of the time
where the time goes in v4:
time: 86.7 us; the launch traced here: 86.6 us
  Pallas kernels  86.6 us (100%)
    pallas_call x1, Pallas kernels, shards(): pl.pallas_call(kernel, out_shape=(pltpu.VMEM((NP - 1, 32, 16, N), BF16),...  83.2 us
    pallas_call x1, Pallas kernels, shards(): pl.pallas_call(finish_kernel, out_shape=jax.ShapeDtypeStruct((32, NP, 16,...  3.4 us

profile of v4, /device:TPU:2, one launch (start us, length us, event | category | flops | bytes accessed | tf_op | source)
XLA Modules:
  0.0 86.6 jit_solution(12428588554382161163)
XLA Ops:
  0.0 83.2 %shard_map.55 = (bf16[7,32,16,1024]{3,2,1,0:T(8,128)(2,1)S(1)}, bf16[2,32,16,512]{3,2,1,0:T(8,128)(2,1)S(1)}, bf16[1024,1024]{1,0:T(8,128)(2,1)S(1)}) custom-call(s32[64]{0:T(128)} %rb_hbm.1, s32[64,64]{1,0:T(8,128)} %mask_hbm.1, bf16[2048,1024]{1,0:T(8,128)(2,1)} %bitcast.3, bf16[64,128]{1,0:T(8,128)(2,1)} %bitcast.4, bf16[1024,1024]{1,0:T(8,128)(2,1)} %vir_hbm.1), custom_call_target="tpu_custom_call" | custom-call | flops 12999999488 | bytes 15728640 | tf_op jit(solution)/shard_map/pallas_call | solution.py:313
  83.2 3.4 %shard_map.56 = bf16[32,8,16,1024]{3,2,1,0:T(8,128)(2,1)} custom-call(bf16[7,32,16,1024]{3,2,1,0:T(8,128)(2,1)S(1)} %get-tuple-element.8.done_ref, bf16[2,32,16,512]{3,2,1,0:T(8,128)(2,1)S(1)} %get-tuple-element.9.last_ref, bf16[1024,1024]{1,0:T(8,128)(2,1)S(1)} %get-tuple-element.10.vir_ref), custom_call_target="tpu_custom_call" | custom-call | tf_op jit(solution)/shard_map/pallas_call | solution.py:346
